TPU v7x, 128 devices: a whole 4x4x4 slice. The times are simulated.
128 devices in a mesh: patch: 8 (over x, core), proto: 16 (over z, y).
Axes of the slice: x: 4, y: 4, z: 4, core: 2. Of those that a mesh axis runs over, the one named last changes fastest.
Arguments:
- student_feats: bfloat16 [32768, 256], P(('patch', 'proto')), may hold values from -50 to 50
- teacher_feats: bfloat16 [32768, 256], P(('patch', 'proto')), may hold values from -50 to 50
- proto_weight: bfloat16 [256, 131072], P(None, 'proto'), may hold values from -4 to 4
- mask_index: int32 [4096], P(('patch', 'proto')), may hold values from 0 to 255, as said below
- row_weight: bfloat16 [4096], P(('patch', 'proto')), may hold values from 0.5 to 4
Outputs:
- grad_student: float32 [4096, 256], P(('patch', 'proto'))
- grad_proto: float32 [256, 131072], P('patch', 'proto')
- loss: float32 [], replicated
Inputs may be any that keep to these rules, and one draw needn't show every extreme that they name: `mask_index`: entries k * 32 to (k + 1) * 32 - 1 are distinct patch positions of image k, counted from that image's first patch.
All inputs are finite; a program needn't handle non-finite values.
Results may differ from a plain program's by a relative error of at most 0.0057.
Values may be sent and summed in bfloat16 or wider, within the bound.
No kernel may reach another device: no remote copies, remote signals or barrier semaphores. Data moves between devices by JAX's collectives and lax.ppermute only.
A program may use at most 128 MiB of HBM per device.

v0:
```python
import jax
import jax.numpy as jnp
from jax import lax
from jax.sharding import PartitionSpec as P

SK_ITERS = 3
eps = 1e-06
teacher_temp = 0.07
student_temp = 0.1


def unit_rows(values):
    values = values.astype(jnp.float32)
    inverse = lax.rsqrt(jnp.sum(values * values, axis=1) + eps)
    return (values * inverse[:, None], inverse)


def finish(teacher_exp, scale_rows, scale_cols, logits, exp_logits, exp_total, weights):
    codes = teacher_exp * scale_rows[:, None] * scale_cols[None, :]
    student_probs = exp_logits / exp_total[:, None]
    grad_logits = (weights[:, None] * (student_probs - codes)).astype(jnp.bfloat16)
    log_total = jnp.log(exp_total)
    loss_partial = jnp.sum(weights[:, None] * codes * (log_total[:, None] - logits))
    return (grad_logits, loss_partial)


def feature_term(grad_logits, proto_cols):
    return (
        lax.dot_general(
            grad_logits, proto_cols, (((1,), (1,)), ((), ())), preferred_element_type=jnp.float32
        )
        / student_temp
    )


def head_term(student_rows, grad_logits):
    return (
        lax.dot_general(
            student_rows, grad_logits, (((0,), (0,)), ((), ())), preferred_element_type=jnp.float32
        )
        / student_temp
    )


def on_device(student_feats, teacher_feats, proto_weight, mask_index, row_weight):
    highest = lax.Precision.HIGHEST
    unit_student, inverse_student = unit_rows(jnp.take(student_feats, mask_index, axis=0))
    unit_teacher, _ = unit_rows(jnp.take(teacher_feats, mask_index, axis=0))
    own_student = unit_student.astype(jnp.bfloat16)
    own_teacher = unit_teacher.astype(jnp.bfloat16)
    w_float = proto_weight.astype(jnp.float32)
    col_inverse = lax.rsqrt(jnp.sum(w_float * w_float, axis=0) + eps)
    unit_proto = w_float * col_inverse[None, :]
    proto_unit = unit_proto.astype(jnp.bfloat16)
    teacher_rows, student_rows, weights = (
        lax.all_gather(own_teacher, "proto", axis=0, tiled=True),
        lax.all_gather(own_student, "proto", axis=0, tiled=True),
        lax.all_gather(row_weight, "proto", axis=0, tiled=True),
    )
    weights = weights.astype(jnp.float32)
    teacher_exp = jnp.exp(
        jnp.dot(teacher_rows, proto_unit, preferred_element_type=jnp.float32) / teacher_temp
    )
    scale_rows = jnp.ones((teacher_rows.shape[0],), jnp.float32)
    for sweep in range(SK_ITERS):
        col_part = jnp.dot(scale_rows, teacher_exp, precision=highest)
        scale_cols = 1.0 / lax.psum(col_part, "patch")
        row_part = jnp.dot(teacher_exp, scale_cols, precision=highest)
        scale_rows = 1.0 / lax.psum(row_part, "proto")
    logits = jnp.dot(student_rows, proto_unit, preferred_element_type=jnp.float32) / student_temp
    exp_logits = jnp.exp(logits)
    exp_total = lax.psum(jnp.sum(exp_logits, axis=1), "proto")
    grad_logits, loss_partial = finish(
        teacher_exp, scale_rows, scale_cols, logits, exp_logits, exp_total, weights
    )
    feature_grad = lax.psum_scatter(
        feature_term(grad_logits, proto_unit), "proto", scatter_dimension=0, tiled=True
    )
    row_share = proto_unit.shape[0] // lax.axis_size("patch")
    row_offset = lax.axis_index("patch") * row_share
    head_full = lax.psum(head_term(student_rows, grad_logits), "patch")
    inner = jnp.sum(unit_proto * head_full, axis=0)
    whole_grad = col_inverse[None, :] * (head_full - unit_proto * inner[None, :])
    grad_proto = lax.dynamic_slice_in_dim(whole_grad, row_offset, row_share, 0)
    loss_total, weight_total = lax.psum(
        (loss_partial, jnp.sum(row_weight.astype(jnp.float32))), ("patch", "proto")
    )
    grad_student = inverse_student[:, None] * (
        feature_grad - unit_student * jnp.sum(unit_student * feature_grad, axis=1)[:, None]
    )
    return (grad_student, grad_proto, loss_total / weight_total)


def solution(mesh):
    in_specs = (
        P(("patch", "proto"), None),
        P(("patch", "proto"), None),
        P(None, "proto"),
        P(("patch", "proto")),
        P(("patch", "proto")),
    )
    out_specs = (P(("patch", "proto"), None), P("patch", "proto"), P())
    return jax.shard_map(
        on_device, mesh=mesh, in_specs=in_specs, out_specs=out_specs, check_vma=False
    )
```

profile of v0, /device:TPU:1, one launch (start us, length us, event | category | flops | bytes accessed | tf_op | source)
XLA Modules:
  0.0 526.8 jit_solution(3142531026962949100)
XLA Ops:
  8.1 0.7 compare_select_fusion
  8.7 0.7 compare_and_fusion
  9.4 0.6 gather_fusion
  10.1 1.5 gather_fusion.1
  11.9 20.8 %all_gather.11 = bf16[512,256]{1,0:T(8,128)(2,1)S(1)} all-gather(bf16[32,256]{1,0:T(8,128)(2,1)S(1)} %get-tuple-element.15), channel_id=1, replica_groups=mesh['patch'=8,'proto'=16] {'proto'}, dimensions={0}, use_global_device_ids=true | all-gather | bytes 278528 | tf_op jit(solution)/shard_map/all_gather | solution.py:56
  32.7 3.1 fusion
  35.8 4.5 multiply_exponential_fusion
  40.3 7.9 %fusion.20 = f32[1,8192]{1,0:T(1,128)S(1)} fusion(f32[512,8192]{1,0:T(8,128)S(1)} %multiply_exponential_fusion), kind=kOutput, calls=%fused_computation.41 | convolution fusion | flops 50331648 | bytes 16809984 | tf_op jit(solution)/shard_map/dot_general | solution.py:66
  48.2 26.1 %psum.71 = f32[8192]{0:T(1024)S(1)} all-reduce(f32[8192]{0:T(1024)S(1)} %bitcast.33), channel_id=1, replica_groups=mesh['patch'=8,'proto'=16] {'patch'}, use_global_device_ids=true, to_apply=%region_5.7 | all-reduce | flops 8192 | bytes 65536 | tf_op jit(solution)/shard_map/psum | solution.py:67
  74.4 17.6 %fusion.23 = f32[1,512]{1,0:T(1,128)S(1)} fusion(f32[512,8192]{1,0:T(8,128)} %copy-done.2, f32[8192,1]{0,1:T(1,128)S(1)} %bitcast.29), kind=kOutput, calls=%fused_computation.50 | convolution fusion | flops 50331648 | bytes 16812032 | tf_op jit(solution)/shard_map/dot_general | solution.py:68
  92.0 31.0 %psum.72 = f32[512]{0:T(512)S(1)} all-reduce(f32[512]{0:T(512)S(1)} %bitcast.35), channel_id=1, replica_groups=mesh['patch'=8,'proto'=16] {'proto'}, use_global_device_ids=true, to_apply=%region_6.8 | all-reduce | flops 512 | bytes 4096 | tf_op jit(solution)/shard_map/psum | solution.py:69
  123.0 11.5 %fusion.24 = f32[1,8192]{1,0:T(1,128)S(1)} fusion(f32[512,1]{0,1:T(1,128)S(1)} %bitcast.37, f32[512,8192]{1,0:T(8,128)} %copy-done.2), kind=kOutput, calls=%fused_computation.51 | convolution fusion | flops 50331648 | bytes 16812032 | tf_op jit(solution)/shard_map/dot_general | solution.py:66
  134.5 30.9 %psum.73 = f32[8192]{0:T(1024)S(1)} all-reduce(f32[8192]{0:T(1024)S(1)} %bitcast.30), channel_id=1, replica_groups=mesh['patch'=8,'proto'=16] {'patch'}, use_global_device_ids=true, to_apply=%region_7.9 | all-reduce | flops 8192 | bytes 65536 | tf_op jit(solution)/shard_map/psum | solution.py:67
  165.4 17.6 %fusion.25 = f32[1,512]{1,0:T(1,128)S(1)} fusion(f32[512,8192]{1,0:T(8,128)} %copy-done.2, f32[8192,1]{0,1:T(1,128)S(1)} %bitcast.31), kind=kOutput, calls=%fused_computation.52 | convolution fusion | flops 50331648 | bytes 16812032 | tf_op jit(solution)/shard_map/dot_general | solution.py:68
  183.0 28.5 %psum.74 = f32[512]{0:T(512)S(1)} all-reduce(f32[512]{0:T(512)S(1)} %bitcast.36), channel_id=1, replica_groups=mesh['patch'=8,'proto'=16] {'proto'}, use_global_device_ids=true, to_apply=%region_8.10 | all-reduce | flops 512 | bytes 4096 | tf_op jit(solution)/shard_map/psum | solution.py:69
  211.5 11.5 %fusion.26 = f32[1,8192]{1,0:T(1,128)S(1)} fusion(f32[512,1]{0,1:T(1,128)S(1)} %bitcast.38, f32[512,8192]{1,0:T(8,128)} %copy-done.2), kind=kOutput, calls=%fused_computation.53 | convolution fusion | flops 50331648 | bytes 16812032 | tf_op jit(solution)/shard_map/dot_general | solution.py:66
  223.0 31.0 %psum.75 = f32[8192]{0:T(1024)S(1)} all-reduce(f32[8192]{0:T(1024)S(1)} %bitcast.32), channel_id=1, replica_groups=mesh['patch'=8,'proto'=16] {'patch'}, use_global_device_ids=true, to_apply=%region_9.11 | all-reduce | flops 8192 | bytes 65536 | tf_op jit(solution)/shard_map/psum | solution.py:67
  254.0 17.8 %fusion.27 = f32[1,512]{1,0:T(1,128)S(1)} fusion(f32[512,8192]{1,0:T(8,128)} %copy-done.2, f32[8192,1]{0,1:T(1,128)S(1)} %bitcast.28), kind=kOutput, calls=%fused_computation.54 | convolution fusion | flops 50331648 | bytes 16812032 | tf_op jit(solution)/shard_map/dot_general | solution.py:68
  271.7 17.8 %all_gather.10 = bf16[512,256]{1,0:T(8,128)(2,1)S(1)} all-gather(bf16[32,256]{1,0:T(8,128)(2,1)S(1)} %get-tuple-element.14), channel_id=1, replica_groups=mesh['patch'=8,'proto'=16] {'proto'}, dimensions={0}, use_global_device_ids=true | all-gather | bytes 278528 | tf_op jit(solution)/shard_map/all_gather | solution.py:57
  289.5 7.5 %exponential_reduce_fusion = (f32[512]{0:T(512)S(1)}, f32[512,8192]{1,0:T(8,128)}) fusion(bf16[512,256]{1,0:T(8,128)(2,1)S(1)} %all_gather.10, f32[8192]{0:T(1024)S(1)} %add_rsqrt_fusion, bf16[256,8192]{1,0:T(8,128)(2,1)S(1)} %copy-done.3), kind=kOutput, calls=%fused_computation.6 | convolution fusion | flops 2162163200 | bytes 21268480 | tf_op jit(solution)/shard_map/dot_general | solution.py:70
  297.0 30.9 %all-reduce.2 = (f32[512]{0:T(512)S(1)}, f32[512]{0:T(512)S(1)}) all-reduce(f32[512]{0:T(512)S(1)} %bitcast.34, f32[512]{0:T(512)S(1)} %get-tuple-element.16), channel_id=1, replica_groups=mesh['patch'=8,'proto'=16] {'proto'}, use_global_device_ids=true, to_apply=%region_10.12 | all-reduce | flops 1024 | bytes 8192 | tf_op jit(solution)/shard_map/psum | solution.py:69
  329.4 29.0 %all-reduce = bf16[512]{0:T(512)(128)(2,1)S(1)} all-reduce(bf16[512]{0:T(512)(128)(2,1)S(1)} %dynamic-update-slice), channel_id=1, replica_groups=mesh['patch'=8,'proto'=16] {'proto'}, use_global_device_ids=true, to_apply=%add | all-reduce | flops 512 | bytes 2048
  358.4 14.4 %multiply_reduce_fusion = (f32[]{:T(128)}, bf16[512,8192]{1,0:T(8,128)(2,1)S(1)}) fusion(f32[512,8192]{1,0:T(8,128)} %copy-done.2, f32[512,8192]{1,0:T(8,128)} %get-tuple-element.17, f32[512]{0:T(512)S(1)} %log.3, f32[8192]{0:T(1024)S(1)} %broadcast_divide_fusion, f32[512]{0:T(512)S(1)} %broadcast_divide_fusion.5, f32[512]{0:T(512)S(1)} %convert_element_type.28, ...), kind=kLoop, calls=%fused_computation.2 | loop fusion | flops 46137344 | bytes 41984004 | tf_op jit(solution)/shard_map/reduce_sum | solution.py:23
  372.9 3.2 copy-done.5
  376.1 3.2 fusion.7
  379.4 9.0 %convolution_multiply_fusion = f32[256,8192]{1,0:T(8,128)} fusion(bf16[512,256]{1,0:T(8,128)(2,1)S(1)} %all_gather.10, bf16[512,8192]{1,0:T(8,128)(2,1)} %copy-done.5), kind=kOutput, calls=%fused_computation.7 | convolution fusion | flops 2149580800 | bytes 17039360 | tf_op jit(solution)/shard_map/dot_general | solution.py:38
  389.0 85.0 %all-reduce.1 = (f32[]{:T(128)}, f32[]{:T(128)}) all-reduce(f32[]{:T(128)} %get-tuple-element.10, f32[]{:T(128)} %convert_reduce_fusion), channel_id=1, replica_groups=mesh['patch'=8,'proto'=16] {'patch','proto'}, use_global_device_ids=true, to_apply=%region_16.18 | all-reduce | flops 2 | bytes 16 | tf_op jit(solution)/shard_map/psum | solution.py:85
  475.3 0.9 fusion.14
  476.3 1.5 fusion.16
  477.8 32.0 %all-reduce.5.cloned.1.call-done = f32[256,8192]{1,0:T(8,128)} async-done(((f32[256,8192]{1,0:T(8,128)}), f32[256,8192]{1,0:T(8,128)}) %all-reduce.5.cloned.1.call-update) | async-done | bytes 8388624 | tf_op jit(solution)/shard_map/psum | solution.py:81
  509.8 6.0 %multiply_reduce_fusion.1 = (f32[8192]{0:T(1024)S(1)}, f32[256,8192]{1,0:T(8,128)S(1)}) fusion(f32[256,8192]{1,0:T(8,128)} %all-reduce.5.cloned.1.call-done, f32[8192]{0:T(1024)S(1)} %add_rsqrt_fusion, bf16[256,8192]{1,0:T(8,128)(2,1)} %param.9), kind=kLoop, calls=%fused_computation.11 | loop fusion | flops 8380416 | bytes 21037056 | tf_op jit(solution)/shard_map/reduce_sum | solution.py:82
  515.7 2.3 fusion.10
  (37 shorter events, 2.0 us)
Async XLA Ops:
  8.0 1.4 copy-start
  8.0 467.3 %reduce-scatter.2.cloned.1.call-start = ((), (), s32[]{:S(2)}) async-start(), calls=%async_computation.1 | async-start | bytes 557056 | tf_op jit(solution)/shard_map/reduce_scatter | solution.py:76
  40.3 8.0 %copy-start.2 = (f32[512,8192]{1,0:T(8,128)}, f32[512,8192]{1,0:T(8,128)S(1)}, u32[]{:S(2)}) copy-start(f32[512,8192]{1,0:T(8,128)S(1)} %multiply_exponential_fusion) | copy-start | bytes 50331652
  253.9 35.6 %copy-start.3 = (bf16[256,8192]{1,0:T(8,128)(2,1)S(1)}, bf16[256,8192]{1,0:T(8,128)(2,1)}, u32[]{:S(2)}) copy-start(bf16[256,8192]{1,0:T(8,128)(2,1)} %param.9) | copy-start | bytes 12582916
  289.5 38.4 %copy-start.7 = (u32[128]{0:T(128)S(1)}, u32[128]{0:T(128)}, u32[]{:S(2)}) copy-start(u32[128]{0:T(128)} %constant.44) | copy-start | bytes 1540
  289.5 39.6 %copy-start.6 = (bf16[32]{0:T(256)(128)(2,1)S(1)}, bf16[32]{0:T(256)(128)(2,1)}, u32[]{:S(2)}) copy-start(bf16[32]{0:T(256)(128)(2,1)} %param.11) | copy-start | bytes 196
  358.4 17.7 %copy-start.4 = (bf16[256,8192]{1,0:T(8,128)(2,1)S(1)}, bf16[256,8192]{1,0:T(8,128)(2,1)}, u32[]{:S(2)}) copy-start(bf16[256,8192]{1,0:T(8,128)(2,1)} %param.9) | copy-start | bytes 12582916
  372.9 3.2 copy-start.5
  379.3 130.5 %all-reduce.5.cloned.1.call-start = ((), (), s32[]{:S(2)}) async-start(), calls=%async_computation.2 | async-start | bytes 16777216 | tf_op jit(solution)/shard_map/psum | solution.py:81
  476.2 41.8 %copy-start.1 = (bf16[256,256]{1,0:T(8,128)(2,1)S(1)}, bf16[256,256]{1,0:T(8,128)(2,1)}, u32[]{:S(2)}) copy-start(bf16[256,256]{1,0:T(8,128)(2,1)} %param.7) | copy-start | bytes 393220
Sparse Core Ops, SparseCore 0:
  379.4 87.7 reduce-scatter.1
Sparse Core Ops, SparseCore 1:
  388.5 121.3 all-reduce.4
where the time goes:
time: 536 us; the launch traced here: 527 us
  blocking collectives  331 us (62%)
  matrix products  108 us (20%)
  waiting for transfers between devices  32.1 us (6%)
  other arithmetic  30.5 us (6%)
  between operations  18.9 us (4%)
  local copies, waits for them, and re-layouts  6.24 us (1%)
    psum x3, blocking collectives, on_device(): scale_rows = 1.0 / lax.psum(row_part, 'proto')  90.4 us
    psum x3, blocking collectives, on_device(): scale_cols = 1.0 / lax.psum(col_part, 'patch')  88 us
    psum x1, blocking collectives, on_device(): lax.psum((loss_partial, jnp.sum(row_weight.astype(jnp.float32))), ('patch...  85 us
    dot_general x3, matrix products, on_device(): row_part = jnp.dot(teacher_exp, scale_cols, precision=highest)  53 us
    psum x1, waiting for transfers between devices, on_device(): head_full = lax.psum(head_term(student_rows, grad_logits), 'patch')  32 us
    dot_general x3, matrix products, on_device(): col_part = jnp.dot(scale_rows, teacher_exp, precision=highest)  30.8 us
    unnamed x1, blocking collectives  29 us
    all_gather x1, blocking collectives, on_device(): lax.all_gather(own_teacher, 'proto', axis=0, tiled=True)  20.8 us
  transfers between devices with their start and end apart: 2, of which 1 were waited for; matrix products, arithmetic and copies ran while one was open for 2% of the time, Pallas kernels for 0%

commit v1 on v0

--- a/solution.py
+++ b/solution.py
@@ -7,6 +7,11 @@
 eps = 1e-06
 teacher_temp = 0.07
 student_temp = 0.1
+
+
+def gather_over(value, axis, dim):
+    outgoing = jnp.stack([value] * lax.axis_size(axis))
+    return jnp.concatenate(lax.all_to_all(outgoing, axis, 0, 0), axis=dim)
 
 
 def unit_rows(values):
@@ -53,7 +58,7 @@
     unit_proto = w_float * col_inverse[None, :]
     proto_unit = unit_proto.astype(jnp.bfloat16)
     teacher_rows, student_rows, weights = (
-        lax.all_gather(own_teacher, "proto", axis=0, tiled=True),
+        gather_over(own_teacher, "proto", 0),
         lax.all_gather(own_student, "proto", axis=0, tiled=True),
         lax.all_gather(row_weight, "proto", axis=0, tiled=True),
     )

time: 536 us -> 518 us (0.966)
  blocking collectives: 331 us -> 306 us
  starting transfers between devices: 0.08 us -> 9.15 us
    all_gather x1 -> x0, blocking collectives: 20.8 us -> none  [on_device(): lax.all_gather(own_teacher, 'proto', axis=0, tiled=True)]
    psum x1, blocking collectives: 85 us -> 73.2 us  [on_device(): lax.psum((loss_partial, jnp.sum(row_weight.astype(jnp.float32))), ('patch...]
    all_to_all x0 -> x1, starting transfers between devices: none -> 8.6 us  [gather_over(): return jnp.concatenate(lax.all_to_all(outgoing, axis, 0, 0), axis=dim)]
    psum x3, blocking collectives: 88 us -> 95.6 us  [on_device(): scale_cols = 1.0 / lax.psum(col_part, 'patch')]
  transfers between devices with their start and end apart: 2 -> 3, of which waited for: 1 -> 1; matrix products, arithmetic and copies ran while one was open for 2% -> 5% of each run, Pallas kernels for 0% -> 0%
where the time goes in v1:
time: 518 us; the launch traced here: 514 us
  blocking collectives  306 us (59%)
  matrix products  110 us (21%)
  waiting for transfers between devices  32 us (6%)
  other arithmetic  30.5 us (6%)
  between operations  18.9 us (4%)
  starting transfers between devices  9.15 us (2%)
  local copies, waits for them, and re-layouts  6.96 us (1%)
    psum x3, blocking collectives, on_device(): scale_cols = 1.0 / lax.psum(col_part, 'patch')  95.6 us
    psum x3, blocking collectives, on_device(): scale_rows = 1.0 / lax.psum(row_part, 'proto')  87.4 us
    psum x1, blocking collectives, on_device(): lax.psum((loss_partial, jnp.sum(row_weight.astype(jnp.float32))), ('patch...  73.2 us
    dot_general x3, matrix products, on_device(): row_part = jnp.dot(teacher_exp, scale_cols, precision=highest)  52.8 us
    psum x1, waiting for transfers between devices, on_device(): head_full = lax.psum(head_term(student_rows, grad_logits), 'patch')  32 us
    unnamed x1, blocking collectives  31.4 us
    dot_general x3, matrix products, on_device(): col_part = jnp.dot(scale_rows, teacher_exp, precision=highest)  30.8 us
    all_gather x1, blocking collectives, on_device(): lax.all_gather(own_student, 'proto', axis=0, tiled=True)  18.6 us
  transfers between devices with their start and end apart: 3, of which 1 were waited for; matrix products, arithmetic and copies ran while one was open for 5% of the time, Pallas kernels for 0%

profile of v1, /device:TPU:1, one launch (start us, length us, event | category | flops | bytes accessed | tf_op | source)
XLA Modules:
  0.0 514.1 jit_solution(8531392583103173211)
XLA Ops:
  8.0 0.7 compare_select_fusion
  8.7 0.7 compare_and_fusion
  10.0 1.5 gather_fusion.1
  11.8 0.7 stack.2
  12.6 8.6 %all-to-all-start = ((bf16[16,32,256]{2,1,0:T(8,128)(2,1)}), bf16[16,32,256]{2,1,0:T(8,128)(2,1)S(1)}, u32[]{:S(2)}, u32[]{:S(2)}) async-start(bf16[16,32,256]{2,1,0:T(8,128)(2,1)} %stack.2), calls=%async_computation | async-start | bytes 524288 | tf_op jit(solution)/shard_map/all_to_all | solution.py:14
  21.2 3.1 fusion
  24.3 18.6 %all_gather.7 = bf16[512,256]{1,0:T(8,128)(2,1)S(1)} all-gather(bf16[32,256]{1,0:T(8,128)(2,1)S(1)} %get-tuple-element.14), channel_id=1, replica_groups=mesh['patch'=8,'proto'=16] {'proto'}, dimensions={0}, use_global_device_ids=true | all-gather | bytes 278528 | tf_op jit(solution)/shard_map/all_gather | solution.py:62
  42.9 10.0 %exponential_reduce_fusion = (f32[512]{0:T(512)S(1)}, f32[512,8192]{1,0:T(8,128)}) fusion(bf16[512,256]{1,0:T(8,128)(2,1)S(1)} %all_gather.7, f32[8192]{0:T(1024)S(1)} %add_rsqrt_fusion, bf16[256,8192]{1,0:T(8,128)(2,1)} %param.9), kind=kOutput, calls=%fused_computation.6 | convolution fusion | flops 2162163200 | bytes 21268480 | tf_op jit(solution)/shard_map/dot_general | solution.py:75
  54.5 31.4 %all-reduce = bf16[512]{0:T(512)(128)(2,1)S(1)} all-reduce(bf16[512]{0:T(512)(128)(2,1)S(1)} %dynamic-update-slice), channel_id=1, replica_groups=mesh['patch'=8,'proto'=16] {'proto'}, use_global_device_ids=true, to_apply=%add | all-reduce | flops 512 | bytes 2048
  85.9 4.4 multiply_exponential_fusion
  90.4 7.9 %fusion.20 = f32[1,8192]{1,0:T(1,128)S(1)} fusion(f32[512,8192]{1,0:T(8,128)S(1)} %multiply_exponential_fusion), kind=kOutput, calls=%fused_computation.41 | convolution fusion | flops 50331648 | bytes 16809984 | tf_op jit(solution)/shard_map/dot_general | solution.py:71
  98.3 33.9 %psum.71 = f32[8192]{0:T(1024)S(1)} all-reduce(f32[8192]{0:T(1024)S(1)} %bitcast.35), channel_id=1, replica_groups=mesh['patch'=8,'proto'=16] {'patch'}, use_global_device_ids=true, to_apply=%region_5.7 | all-reduce | flops 8192 | bytes 65536 | tf_op jit(solution)/shard_map/psum | solution.py:72
  132.2 17.6 %fusion.23 = f32[1,512]{1,0:T(1,128)S(1)} fusion(f32[512,8192]{1,0:T(8,128)} %copy-done.2, f32[8192,1]{0,1:T(1,128)S(1)} %bitcast.31), kind=kOutput, calls=%fused_computation.50 | convolution fusion | flops 50331648 | bytes 16812032 | tf_op jit(solution)/shard_map/dot_general | solution.py:73
  149.9 28.5 %psum.72 = f32[512]{0:T(512)S(1)} all-reduce(f32[512]{0:T(512)S(1)} %bitcast.37), channel_id=1, replica_groups=mesh['patch'=8,'proto'=16] {'proto'}, use_global_device_ids=true, to_apply=%region_6.8 | all-reduce | flops 512 | bytes 4096 | tf_op jit(solution)/shard_map/psum | solution.py:74
  178.4 11.5 %fusion.24 = f32[1,8192]{1,0:T(1,128)S(1)} fusion(f32[512,1]{0,1:T(1,128)S(1)} %bitcast.39, f32[512,8192]{1,0:T(8,128)} %copy-done.2), kind=kOutput, calls=%fused_computation.51 | convolution fusion | flops 50331648 | bytes 16812032 | tf_op jit(solution)/shard_map/dot_general | solution.py:71
  189.8 30.8 %psum.73 = f32[8192]{0:T(1024)S(1)} all-reduce(f32[8192]{0:T(1024)S(1)} %bitcast.32), channel_id=1, replica_groups=mesh['patch'=8,'proto'=16] {'patch'}, use_global_device_ids=true, to_apply=%region_7.9 | all-reduce | flops 8192 | bytes 65536 | tf_op jit(solution)/shard_map/psum | solution.py:72
  220.6 17.6 %fusion.25 = f32[1,512]{1,0:T(1,128)S(1)} fusion(f32[512,8192]{1,0:T(8,128)} %copy-done.2, f32[8192,1]{0,1:T(1,128)S(1)} %bitcast.33), kind=kOutput, calls=%fused_computation.52 | convolution fusion | flops 50331648 | bytes 16812032 | tf_op jit(solution)/shard_map/dot_general | solution.py:73
  238.2 30.4 %psum.74 = f32[512]{0:T(512)S(1)} all-reduce(f32[512]{0:T(512)S(1)} %bitcast.38), channel_id=1, replica_groups=mesh['patch'=8,'proto'=16] {'proto'}, use_global_device_ids=true, to_apply=%region_8.10 | all-reduce | flops 512 | bytes 4096 | tf_op jit(solution)/shard_map/psum | solution.py:74
  268.6 11.5 %fusion.26 = f32[1,8192]{1,0:T(1,128)S(1)} fusion(f32[512,1]{0,1:T(1,128)S(1)} %bitcast.40, f32[512,8192]{1,0:T(8,128)} %copy-done.2), kind=kOutput, calls=%fused_computation.53 | convolution fusion | flops 50331648 | bytes 16812032 | tf_op jit(solution)/shard_map/dot_general | solution.py:71
  280.0 30.9 %psum.75 = f32[8192]{0:T(1024)S(1)} all-reduce(f32[8192]{0:T(1024)S(1)} %bitcast.34), channel_id=1, replica_groups=mesh['patch'=8,'proto'=16] {'patch'}, use_global_device_ids=true, to_apply=%region_9.11 | all-reduce | flops 8192 | bytes 65536 | tf_op jit(solution)/shard_map/psum | solution.py:72
  311.0 17.6 %fusion.27 = f32[1,512]{1,0:T(1,128)S(1)} fusion(f32[512,8192]{1,0:T(8,128)} %copy-done.2, f32[8192,1]{0,1:T(1,128)S(1)} %bitcast.30), kind=kOutput, calls=%fused_computation.54 | convolution fusion | flops 50331648 | bytes 16812032 | tf_op jit(solution)/shard_map/dot_general | solution.py:73
  328.6 28.5 %all-reduce.2 = (f32[512]{0:T(512)S(1)}, f32[512]{0:T(512)S(1)}) all-reduce(f32[512]{0:T(512)S(1)} %bitcast.36, f32[512]{0:T(512)S(1)} %get-tuple-element.16), channel_id=1, replica_groups=mesh['patch'=8,'proto'=16] {'proto'}, use_global_device_ids=true, to_apply=%region_10.12 | all-reduce | flops 1024 | bytes 8192 | tf_op jit(solution)/shard_map/psum | solution.py:74
  357.1 14.4 %multiply_reduce_fusion = (f32[]{:T(128)}, bf16[512,8192]{1,0:T(8,128)(2,1)S(1)}) fusion(f32[512,8192]{1,0:T(8,128)} %copy-done.2, f32[512,8192]{1,0:T(8,128)} %get-tuple-element.17, f32[512]{0:T(512)S(1)} %log.3, f32[8192]{0:T(1024)S(1)} %broadcast_divide_fusion, f32[512]{0:T(512)S(1)} %broadcast_divide_fusion.5, f32[512]{0:T(512)S(1)} %convert_element_type.28, ...), kind=kLoop, calls=%fused_computation.2 | loop fusion | flops 46137344 | bytes 41984004 | tf_op jit(solution)/shard_map/reduce_sum | solution.py:28
  371.6 3.2 copy-done.4
  374.8 3.2 fusion.7
  378.5 9.0 %convolution_multiply_fusion = f32[256,8192]{1,0:T(8,128)} fusion(bf16[512,256]{1,0:T(8,128)(2,1)S(1)} %all_gather.7, bf16[512,8192]{1,0:T(8,128)(2,1)} %copy-done.4), kind=kOutput, calls=%fused_computation.7 | convolution fusion | flops 2149580800 | bytes 17039360 | tf_op jit(solution)/shard_map/dot_general | solution.py:43
  388.1 73.2 %all-reduce.1 = (f32[]{:T(128)}, f32[]{:T(128)}) all-reduce(f32[]{:T(128)} %get-tuple-element.10, f32[]{:T(128)} %convert_reduce_fusion), channel_id=1, replica_groups=mesh['patch'=8,'proto'=16] {'patch','proto'}, use_global_device_ids=true, to_apply=%region_16.18 | all-reduce | flops 2 | bytes 16 | tf_op jit(solution)/shard_map/psum | solution.py:90
  462.7 0.9 fusion.14
  463.6 1.5 fusion.16
  465.1 32.0 %all-reduce.5.cloned.1.call-done = f32[256,8192]{1,0:T(8,128)} async-done(((f32[256,8192]{1,0:T(8,128)}), f32[256,8192]{1,0:T(8,128)}) %all-reduce.5.cloned.1.call-update) | async-done | bytes 8388624 | tf_op jit(solution)/shard_map/psum | solution.py:86
  497.1 6.0 %multiply_reduce_fusion.1 = (f32[8192]{0:T(1024)S(1)}, f32[256,8192]{1,0:T(8,128)S(1)}) fusion(f32[256,8192]{1,0:T(8,128)} %all-reduce.5.cloned.1.call-done, f32[8192]{0:T(1024)S(1)} %add_rsqrt_fusion, bf16[256,8192]{1,0:T(8,128)(2,1)} %param.9), kind=kLoop, calls=%fused_computation.11 | loop fusion | flops 8380416 | bytes 21037056 | tf_op jit(solution)/shard_map/reduce_sum | solution.py:87
  503.1 2.3 fusion.10
  (37 shorter events, 3.1 us)
Async XLA Ops:
  8.0 1.4 copy-start
  12.6 73.3 %all-to-all-start = ((bf16[16,32,256]{2,1,0:T(8,128)(2,1)}), bf16[16,32,256]{2,1,0:T(8,128)(2,1)S(1)}, u32[]{:S(2)}, u32[]{:S(2)}) async-start(bf16[16,32,256]{2,1,0:T(8,128)(2,1)} %stack.2), calls=%async_computation | async-start | bytes 524288 | tf_op jit(solution)/shard_map/all_to_all | solution.py:14
  21.2 441.5 %reduce-scatter.2.cloned.1.call-start = ((), (), s32[]{:S(2)}) async-start(), calls=%async_computation.2 | async-start | bytes 557056 | tf_op jit(solution)/shard_map/reduce_scatter | solution.py:81
  42.9 10.1 %copy-start.6 = (u32[128]{0:T(128)S(1)}, u32[128]{0:T(128)}, u32[]{:S(2)}) copy-start(u32[128]{0:T(128)} %constant.44) | copy-start | bytes 1540
  42.9 11.3 %copy-start.5 = (bf16[32]{0:T(256)(128)(2,1)S(1)}, bf16[32]{0:T(256)(128)(2,1)}, u32[]{:S(2)}) copy-start(bf16[32]{0:T(256)(128)(2,1)} %param.11) | copy-start | bytes 196
  90.3 8.0 %copy-start.2 = (f32[512,8192]{1,0:T(8,128)}, f32[512,8192]{1,0:T(8,128)S(1)}, u32[]{:S(2)}) copy-start(f32[512,8192]{1,0:T(8,128)S(1)} %multiply_exponential_fusion) | copy-start | bytes 50331652
  357.1 17.7 %copy-start.3 = (bf16[256,8192]{1,0:T(8,128)(2,1)S(1)}, bf16[256,8192]{1,0:T(8,128)(2,1)}, u32[]{:S(2)}) copy-start(bf16[256,8192]{1,0:T(8,128)(2,1)} %param.9) | copy-start | bytes 12582916
  371.6 3.2 copy-start.4
  378.0 119.1 %all-reduce.5.cloned.1.call-start = ((), (), s32[]{:S(2)}) async-start(), calls=%async_computation.3 | async-start | bytes 16777216 | tf_op jit(solution)/shard_map/psum | solution.py:86
  463.6 41.8 %copy-start.1 = (bf16[256,256]{1,0:T(8,128)(2,1)S(1)}, bf16[256,256]{1,0:T(8,128)(2,1)}, u32[]{:S(2)}) copy-start(bf16[256,256]{1,0:T(8,128)(2,1)} %param.7) | copy-start | bytes 393220
Sparse Core Ops, SparseCore 0:
  378.1 75.9 reduce-scatter.1
Sparse Core Ops, SparseCore 1:
  387.6 109.5 all-reduce.4
